TPU v7x, 128 devices: a whole 4x4x4 slice. The times are simulated.
128 devices in a mesh: dp: 4 (over y_lo, core), expert: 32 (over z, x, y_hi).
Axes of the slice: x: 4, y: 4 (y_hi: 2, y_lo: 2; y = y_hi * 2 + y_lo), z: 4, core: 2. Of those that a mesh axis runs over, the one named last changes fastest.
Arguments:
- hidden: bfloat16 [2048, 4096], P(('dp', 'expert')), may hold values from -6 to 6
- expert_ids: int32 [2048, 8], P(('dp', 'expert')), may hold values from 0 to 31, all different within a row; in each aligned block of 16 rows (0 to 15, 16 to 31, ...) at most 4 rows name the same one
- router_scores: float32 [2048, 8], P(('dp', 'expert')), may hold values from 0.05 to 1
- partner: int32 [32], replicated, may hold values from 0 to 31, as said below
- w_gate: bfloat16 [32, 4096, 1536], P('expert', None, 'dp'), may hold values from -0.09375 to 0.09375
- w_up: bfloat16 [32, 4096, 1536], P('expert', None, 'dp'), may hold values from -0.09375 to 0.09375
- w_down: bfloat16 [32, 4096, 1536], P('expert', None, 'dp'), may hold values from -0.15625 to 0.15625
Outputs:
- mixed: bfloat16 [2048, 4096], P(('dp', 'expert'))
- moved_gate: bfloat16 [32, 4096, 1536], P('expert', None, 'dp')
- moved_up: bfloat16 [32, 4096, 1536], P('expert', None, 'dp')
- moved_down: bfloat16 [32, 4096, 1536], P('expert', None, 'dp')
Inputs may be any that keep to these rules, and one draw needn't show every extreme that they name: `expert_ids`: within the 16 rows of one device no expert is named by more than 4 rows, a bound that some block reaches. partner pairs the slots: partner[partner[t]] = t and partner[t] != t.
All inputs are finite; a program needn't handle non-finite values.
Results may differ from a plain program's by a relative error of at most 0.0058.
Values may be sent and summed in bfloat16 or wider, within the bound.
No kernel may reach another device: no remote copies, remote signals or barrier semaphores. Data moves between devices by JAX's collectives and lax.ppermute only.
A program may use at most 128 MiB of HBM per device.

v0:
```python
import jax
import jax.numpy as jnp
from jax import lax
from jax.sharding import PartitionSpec as P


def shortened(array):

    def short(part):
        return part.astype(jnp.bfloat16) if part.dtype == jnp.float32 else part

    return jax.tree.map(short, array)


def expert_rows(rows, gate_block, up_block, down_block):
    shape = rows.shape
    flat = rows.reshape(-1, shape[-1])
    gate = jnp.dot(flat, gate_block, preferred_element_type=jnp.float32)
    upper = jnp.dot(flat, up_block, preferred_element_type=jnp.float32)
    inner = (jax.nn.silu(gate) * upper).astype(jnp.bfloat16)
    output = lax.dot_general(
        inner, down_block, (((1,), (1,)), ((), ())), preferred_element_type=jnp.float32
    )
    return output.astype(jnp.bfloat16).reshape(shape)


def local(hidden, expert_ids, router_scores, partner, w_gate, w_up, w_down):
    experts = lax.axis_size("expert")
    groups = lax.axis_size("dp")
    rows_here = hidden.shape[0]
    width = hidden.shape[1]
    choose = expert_ids.shape[1]
    capacity = min(rows_here, rows_here * choose * 9 // (8 * experts))
    spread = (
        lax.all_to_all(w_gate, "expert", split_axis=1, concat_axis=0, tiled=True),
        lax.all_to_all(w_up, "expert", split_axis=1, concat_axis=0, tiled=True),
        lax.all_to_all(w_down, "expert", split_axis=1, concat_axis=0, tiled=True),
    )
    routed = tuple((jnp.take(piece, partner, axis=0) for piece in spread))
    moved_gate, moved_up, moved_down = jax.tree.map(
        lambda part, own: part.astype(own.dtype),
        lax.all_to_all(shortened(routed), "expert", split_axis=0, concat_axis=1, tiled=True),
        routed,
    )
    row_weights = router_scores / jnp.sum(router_scores, axis=1, keepdims=True)
    slots_all = jnp.arange(experts, dtype=jnp.int32)
    target = jnp.sum(
        jnp.where(expert_ids[:, :, None] == slots_all, partner[None, None, :], 0), axis=2
    )
    blocks = (moved_gate[0], moved_up[0], moved_down[0])
    flat_target = target.reshape(-1)
    onehot = (flat_target[:, None] == slots_all[None, :]).astype(jnp.int32)
    before = jnp.cumsum(onehot, axis=0) - onehot
    slot = jnp.sum(before * onehot, axis=1)
    position = flat_target * capacity + slot
    columns = jnp.arange(experts * capacity, dtype=jnp.int32)
    hits = (position[:, None] == columns[None, :]).reshape(rows_here, choose, experts * capacity)
    placing = jnp.any(hits, axis=1).astype(jnp.bfloat16)
    combining = jnp.sum(jnp.where(hits, row_weights[:, :, None], jnp.float32(0.0)), axis=1)
    buffer = lax.dot_general(
        placing, hidden, (((0,), (0,)), ((), ())), preferred_element_type=jnp.float32
    )
    buffer = buffer.astype(jnp.bfloat16).reshape(experts, capacity, width)
    outgoing = jnp.tile(buffer, (groups, 1, 1))
    parts = expert_rows(
        lax.all_to_all(outgoing, ("dp", "expert"), split_axis=0, concat_axis=0, tiled=True),
        blocks[0],
        blocks[1],
        blocks[2],
    )
    returned = lax.all_to_all(parts, ("dp", "expert"), split_axis=0, concat_axis=0, tiled=True)
    summed = jnp.sum(
        returned.reshape(groups, experts * capacity, width).astype(jnp.float32), axis=0
    )
    mixed = jnp.dot(
        combining, summed, precision=lax.Precision.HIGHEST, preferred_element_type=jnp.float32
    )
    return (mixed.astype(jnp.bfloat16), moved_gate, moved_up, moved_down)


def solution(mesh):
    placed = (
        P(("dp", "expert"), None),
        P(("dp", "expert"), None),
        P(("dp", "expert"), None),
        P(),
        P("expert", None, "dp"),
        P("expert", None, "dp"),
        P("expert", None, "dp"),
    )
    return jax.shard_map(
        local,
        mesh=mesh,
        in_specs=placed,
        out_specs=(
            P(("dp", "expert"), None),
            P("expert", None, "dp"),
            P("expert", None, "dp"),
            P("expert", None, "dp"),
        ),
        check_vma=False,
    )
```

profile of v0, /device:TPU:1, one launch (start us, length us, event | category | flops | bytes accessed | tf_op | source)
XLA Modules:
  0.0 653.6 jit_solution(17730282679948041627)
XLA Ops:
  0.6 0.0 copy-start
  0.6 6.9 %copy.38 = bf16[1,4096,384]{2,0,1:T(2,128)(2,1)} copy(bf16[1,4096,384]{2,1,0:T(8,128)(2,1)} %param.13) | data formatting | bytes 6291456 | tf_op args[4]
  7.6 0.5 broadcast.33
  8.1 66.9 %reduce = bf16[4096,384]{1,0:T(8,128)(2,1)S(1)} reduce(bf16[4096,1,384]{2,1,0:T(2,128)(2,1)} %bitcast.31, bf16[]{:T(256)} %broadcast.33), dimensions={1}, to_apply=%bitcast.30.reduce_sub_computation | reduce | bytes 6291458
  75.0 2.5 reshape.113
  77.5 11.5 %all-to-all-start.1 = ((bf16[32,2,24576]{2,1,0:T(2,128)(2,1)}), bf16[32,2,24576]{2,1,0:T(2,128)(2,1)S(1)}, u32[]{:S(2)}, u32[]{:S(2)}) async-start(bf16[32,2,24576]{2,1,0:T(2,128)(2,1)} %reshape.113), calls=%async_computation.1 | async-start | bytes 6291456 | tf_op jit(solution)/shard_map/all_to_all | solution.py:35
  89.0 6.9 %copy.37 = bf16[1,4096,384]{2,0,1:T(2,128)(2,1)} copy(bf16[1,4096,384]{2,1,0:T(8,128)(2,1)} %param.14) | data formatting | bytes 6291456 | tf_op args[5]
  95.9 68.6 %reduce.1 = bf16[4096,384]{1,0:T(8,128)(2,1)} reduce(bf16[4096,1,384]{2,1,0:T(2,128)(2,1)} %bitcast.36, bf16[]{:T(256)} %broadcast.33), dimensions={1}, to_apply=%bitcast.29.reduce_sub_computation | reduce | bytes 6291458
  164.5 7.6 %reshape.111 = bf16[32,2,24576]{2,1,0:T(2,128)(2,1)} reshape(bf16[4096,384]{1,0:T(8,128)(2,1)} %reduce.1) | data formatting | bytes 6291456
  172.1 0.0 all-to-all-done.1
  172.1 9.7 %all-to-all-start.3 = ((bf16[32,2,24576]{2,1,0:T(2,128)(2,1)}), bf16[32,2,24576]{2,1,0:T(2,128)(2,1)}, u32[]{:S(2)}, u32[]{:S(2)}) async-start(bf16[32,2,24576]{2,1,0:T(2,128)(2,1)} %reshape.111), calls=%async_computation.3 | async-start | bytes 6291456 | tf_op jit(solution)/shard_map/all_to_all | solution.py:36
  181.8 6.9 %copy.36 = bf16[1,4096,384]{2,0,1:T(2,128)(2,1)} copy(bf16[1,4096,384]{2,1,0:T(8,128)(2,1)} %param.15) | data formatting | bytes 6291456 | tf_op args[6]
  188.7 68.6 %reduce.2 = bf16[4096,384]{1,0:T(8,128)(2,1)} reduce(bf16[4096,1,384]{2,1,0:T(2,128)(2,1)} %bitcast.32, bf16[]{:T(256)} %broadcast.33), dimensions={1}, to_apply=%bitcast.28.reduce_sub_computation | reduce | bytes 6291458
  257.3 7.6 %reshape.109 = bf16[32,2,24576]{2,1,0:T(2,128)(2,1)} reshape(bf16[4096,384]{1,0:T(8,128)(2,1)} %reduce.2) | data formatting | bytes 6291456
  264.8 0.0 all-to-all-done.3
  264.8 9.6 %all-to-all-start.5 = ((bf16[32,2,24576]{2,1,0:T(2,128)(2,1)}), bf16[32,2,24576]{2,1,0:T(2,128)(2,1)}, u32[]{:S(2)}, u32[]{:S(2)}) async-start(bf16[32,2,24576]{2,1,0:T(2,128)(2,1)} %reshape.109), calls=%async_computation.5 | async-start | bytes 6291456 | tf_op jit(solution)/shard_map/all_to_all | solution.py:37
  274.4 0.0 copy-done.5
  274.5 0.1 copy.25
  274.5 0.0 copy-done.6
  274.5 0.4 select_reduce_fusion.2
  274.9 0.1 eq.45
  275.0 0.1 fusion.3
  275.1 0.2 reduce_window_sum.11
  275.3 0.2 select_reduce_fusion.1
  275.5 0.1 reduce_sum.49
  275.6 0.1 fusion.2
  275.7 0.0 copy-done
  275.7 1.5 convolution_convert_fusion.1
  277.2 2.2 tile.10
  279.4 36.6 %all-to-all-done.5 = bf16[32,2,24576]{2,1,0:T(2,128)(2,1)} async-done(((bf16[32,2,24576]{2,1,0:T(2,128)(2,1)}), bf16[32,2,24576]{2,1,0:T(2,128)(2,1)}, u32[]{:S(2)}, u32[]{:S(2)}) %all-to-all-start.5) | async-done | bytes 3145760 | tf_op jit(solution)/shard_map/all_to_all | solution.py:37
  316.0 5.4 tile.11
  321.4 8.2 %all-to-all-start = ((bf16[128,4,4096]{2,1,0:T(4,128)(2,1)}), bf16[128,4,4096]{2,1,0:T(4,128)(2,1)}, u32[]{:S(2)}, u32[]{:S(2)}) async-start(bf16[128,4,4096]{2,1,0:T(4,128)(2,1)} %bitcast.37), calls=%async_computation | async-start | bytes 8388608 | tf_op jit(solution)/shard_map/all_to_all | solution.py:66
  329.7 12.4 %reshape.114 = bf16[4096,1,384]{2,1,0:T(2,128)(2,1)} reshape(bf16[32,2,24576]{2,1,0:T(2,128)(2,1)S(1)} %all-to-all-done.1) | data formatting | bytes 6291456
  342.1 3.3 copy.30
  345.4 18.9 %reshape.112 = bf16[4096,1,384]{2,1,0:T(2,128)(2,1)} reshape(bf16[32,2,24576]{2,1,0:T(2,128)(2,1)} %all-to-all-done.3) | data formatting | bytes 6291456
  364.3 5.0 copy.31
  369.3 2.6 gather_fusion
  371.9 4.5 gather_fusion.1
  376.5 18.9 %reshape.110 = bf16[4096,1,384]{2,1,0:T(2,128)(2,1)} reshape(bf16[32,2,24576]{2,1,0:T(2,128)(2,1)} %all-to-all-done.5) | data formatting | bytes 6291456
  395.4 3.3 copy.32
  398.7 2.6 gather_fusion.2
  401.3 6.5 broadcast_select_fusion.2
  407.8 0.0 all-to-all-done
  407.8 51.3 %all_to_all.82 = bf16[32,128,384]{2,1,0:T(8,128)(2,1)S(1)} all-to-all(bf16[32,128,384]{2,1,0:T(8,128)(2,1)} %get-tuple-element.5), channel_id=1, replica_groups=mesh['dp'=4,'expert'=32] {'expert'}, dimensions={0} | all-to-all | bytes 6291456 | tf_op jit(solution)/shard_map/all_to_all | solution.py:42
  459.1 0.0 copy-done.3
  459.1 43.7 %all_to_all.83 = bf16[32,128,384]{2,1,0:T(8,128)(2,1)} all-to-all(bf16[32,128,384]{2,1,0:T(8,128)(2,1)S(1)} %copy-done.3), channel_id=1, replica_groups=mesh['dp'=4,'expert'=32] {'expert'}, dimensions={0} | all-to-all | bytes 6291456 | tf_op jit(solution)/shard_map/all_to_all | solution.py:42
  502.8 4.8 all-to-all-start.6
  507.6 6.9 %reshape.73 = bf16[512,4096]{1,0:T(8,128)(2,1)} reshape(bf16[128,4,4096]{2,1,0:T(4,128)(2,1)} %all-to-all-done) | data formatting | bytes 8388608 | tf_op jit(solution)/shard_map/reshape | solution.py:17
  514.5 5.4 fusion.5
  519.9 28.0 %all-to-all-done.6 = bf16[32,128,384]{2,1,0:T(8,128)(2,1)} async-done(((bf16[32,128,384]{2,1,0:T(8,128)(2,1)}), bf16[32,128,384]{2,1,0:T(8,128)(2,1)}, u32[]{:S(2)}, u32[]{:S(2)}) %all-to-all-start.6) | async-done | bytes 3145760 | tf_op jit(solution)/shard_map/all_to_all | solution.py:42
  547.9 10.7 %convolution_convert_fusion = bf16[512,4096]{1,0:T(8,128)(2,1)} fusion(bf16[4096,384]{1,0:T(8,128)(2,1)} %bitcast.3, bf16[512,4096]{1,0:T(8,128)(2,1)} %reshape.73, bf16[4096,384]{1,0:T(8,128)(2,1)} %bitcast.40, f32[512,384]{1,0:T(8,128)} %fusion.5), kind=kOutput, calls=%fused_computation.3 | convolution fusion | flops 3224502272 | bytes 15466496 | tf_op jit(solution)/shard_map/dot_general | solution.py:21
  558.6 7.2 %reshape.74 = bf16[128,4,4096]{2,1,0:T(4,128)(2,1)} reshape(bf16[512,4096]{1,0:T(8,128)(2,1)} %convolution_convert_fusion) | data formatting | bytes 8388608 | tf_op jit(solution)/shard_map/reshape | solution.py:24
  565.8 10.3 %all-to-all-start.7 = ((bf16[128,4,4096]{2,1,0:T(4,128)(2,1)}), bf16[128,4,4096]{2,1,0:T(4,128)(2,1)}, u32[]{:S(2)}, u32[]{:S(2)}) async-start(bf16[128,4,4096]{2,1,0:T(4,128)(2,1)} %reshape.74), calls=%async_computation.7 | async-start | bytes 8388608 | tf_op jit(solution)/shard_map/all_to_all | solution.py:71
  576.2 0.0 copy-done.4
  576.2 0.1 copy.26
  576.3 0.1 select_reduce_fusion
  576.4 52.1 %all-to-all-done.7 = bf16[128,4,4096]{2,1,0:T(4,128)(2,1)} async-done(((bf16[128,4,4096]{2,1,0:T(4,128)(2,1)}), bf16[128,4,4096]{2,1,0:T(4,128)(2,1)}, u32[]{:S(2)}, u32[]{:S(2)}) %all-to-all-start.7) | async-done | bytes 4194336 | tf_op jit(solution)/shard_map/all_to_all | solution.py:71
  628.5 7.3 %reshape.75 = f32[4,128,4096]{2,1,0:T(8,128)} reshape(bf16[128,4,4096]{2,1,0:T(4,128)(2,1)} %all-to-all-done.7) | data formatting | bytes 12582912 | tf_op jit(solution)/shard_map/convert_element_type | solution.py:73
  635.7 5.5 reduce_sum.52
  641.2 3.3 convolution_convert_fusion.2
  644.6 1.7 copy.42
  646.2 1.4 copy-done.2
  647.6 1.7 copy.43
  649.3 3.9 copy.44
  (13 shorter events, 0.1 us)
Async XLA Ops:
  0.6 275.1 %copy-start = (bf16[16,4096]{1,0:T(8,128)(2,1)S(1)}, bf16[16,4096]{1,0:T(8,128)(2,1)}, u32[]{:S(2)}) copy-start(bf16[16,4096]{1,0:T(8,128)(2,1)} %param.9) | copy-start | bytes 393220
  77.5 94.6 %all-to-all-start.1 = ((bf16[32,2,24576]{2,1,0:T(2,128)(2,1)}), bf16[32,2,24576]{2,1,0:T(2,128)(2,1)S(1)}, u32[]{:S(2)}, u32[]{:S(2)}) async-start(bf16[32,2,24576]{2,1,0:T(2,128)(2,1)} %reshape.113), calls=%async_computation.1 | async-start | bytes 6291456 | tf_op jit(solution)/shard_map/all_to_all | solution.py:35
  172.1 92.7 %all-to-all-start.3 = ((bf16[32,2,24576]{2,1,0:T(2,128)(2,1)}), bf16[32,2,24576]{2,1,0:T(2,128)(2,1)}, u32[]{:S(2)}, u32[]{:S(2)}) async-start(bf16[32,2,24576]{2,1,0:T(2,128)(2,1)} %reshape.111), calls=%async_computation.3 | async-start | bytes 6291456 | tf_op jit(solution)/shard_map/all_to_all | solution.py:36
  264.8 9.6 %copy-start.5 = (s32[16,8]{0,1:T(8,128)S(1)}, s32[16,8]{0,1:T(8,128)}, u32[]{:S(2)}) copy-start(s32[16,8]{0,1:T(8,128)} %param.10) | copy-start | bytes 1540
  264.8 9.7 %copy-start.6 = (s32[32]{0:T(128)S(1)}, s32[32]{0:T(128)}, u32[]{:S(2)}) copy-start(s32[32]{0:T(128)} %param.12) | copy-start | bytes 388
  264.8 51.2 %all-to-all-start.5 = ((bf16[32,2,24576]{2,1,0:T(2,128)(2,1)}), bf16[32,2,24576]{2,1,0:T(2,128)(2,1)}, u32[]{:S(2)}, u32[]{:S(2)}) async-start(bf16[32,2,24576]{2,1,0:T(2,128)(2,1)} %reshape.109), calls=%async_computation.5 | async-start | bytes 6291456 | tf_op jit(solution)/shard_map/all_to_all | solution.py:37
  321.4 86.4 %all-to-all-start = ((bf16[128,4,4096]{2,1,0:T(4,128)(2,1)}), bf16[128,4,4096]{2,1,0:T(4,128)(2,1)}, u32[]{:S(2)}, u32[]{:S(2)}) async-start(bf16[128,4,4096]{2,1,0:T(4,128)(2,1)} %bitcast.37), calls=%async_computation | async-start | bytes 8388608 | tf_op jit(solution)/shard_map/all_to_all | solution.py:66
  407.8 51.3 %copy-start.3 = (bf16[32,128,384]{2,1,0:T(8,128)(2,1)S(1)}, bf16[32,128,384]{2,1,0:T(8,128)(2,1)}, u32[]{:S(2)}) copy-start(bf16[32,128,384]{2,1,0:T(8,128)(2,1)} %get-tuple-element.6) | copy-start | bytes 9437188
  502.8 45.1 %all-to-all-start.6 = ((bf16[32,128,384]{2,1,0:T(8,128)(2,1)}), bf16[32,128,384]{2,1,0:T(8,128)(2,1)}, u32[]{:S(2)}, u32[]{:S(2)}) async-start(bf16[32,128,384]{2,1,0:T(8,128)(2,1)} %get-tuple-element.7), calls=%async_computation.6 | async-start | bytes 6291456 | tf_op jit(solution)/shard_map/all_to_all | solution.py:42
  565.8 10.3 %copy-start.4 = (f32[16,8]{0,1:T(8,128)S(1)}, f32[16,8]{0,1:T(8,128)}, u32[]{:S(2)}) copy-start(f32[16,8]{0,1:T(8,128)} %param.11) | copy-start | bytes 1540
  565.8 62.6 %all-to-all-start.7 = ((bf16[128,4,4096]{2,1,0:T(4,128)(2,1)}), bf16[128,4,4096]{2,1,0:T(4,128)(2,1)}, u32[]{:S(2)}, u32[]{:S(2)}) async-start(bf16[128,4,4096]{2,1,0:T(4,128)(2,1)} %reshape.74), calls=%async_computation.7 | async-start | bytes 8388608 | tf_op jit(solution)/shard_map/all_to_all | solution.py:71
  644.6 3.0 copy-start.2
  647.6 5.5 copy-start.1
where the time goes:
time: 663 us; the launch traced here: 654 us
  other arithmetic  217 us (33%)
  local copies, waits for them, and re-layouts  148 us (22%)
  waiting for transfers between devices  117 us (18%)
  blocking collectives  95 us (14%)
  starting transfers between devices  54.2 us (8%)
  matrix products  20.9 us (3%)
    unnamed x3, other arithmetic  204 us
    unnamed x31, local copies, waits for them, and re-layouts  109 us
    all_to_all x2, blocking collectives, local(): lax.all_to_all(shortened(routed), 'expert', split_axis=0, concat_axis=1,...  95 us
    all_to_all x1, waiting for transfers between devices, local(): lax.all_to_all(parts, ('dp', 'expert'), split_axis=0, concat_axis=0, tile...  52.1 us
    all_to_all x1, waiting for transfers between devices, local(): lax.all_to_all(w_down, 'expert', split_axis=1, concat_axis=0, tiled=True)  36.6 us
    all_to_all x1, waiting for transfers between devices, local(): lax.all_to_all(shortened(routed), 'expert', split_axis=0, concat_axis=1,...  28 us
  transfers between devices with their start and end apart: 6, of which 3 were waited for; matrix products, arithmetic and copies ran while one was open for 40% of the time, Pallas kernels for 0%

commit v1 on v0

v1 whole, which is shorter than its diff:
```python
import jax
import jax.numpy as jnp
from jax import lax
from jax.sharding import PartitionSpec as P

NZ, NX, NY = 4, 4, 2
SLOTS = 8


def expert_perm(dz, dx, dy):
    pairs = []
    for i in range(NZ * NX * NY):
        z, x, y = i // (NX * NY), (i // NY) % NX, i % NY
        j = ((z + dz) % NZ) * NX * NY + ((x + dx) % NX) * NY + (y + dy) % NY
        pairs.append((i, j))
    return pairs


def along_z(part, step):
    return lax.ppermute(part, "expert", expert_perm(step, 0, 0))


def along_x(part, step):
    return lax.ppermute(part, "expert", expert_perm(0, step, 0))


def along_y(part):
    return lax.ppermute(part, "expert", expert_perm(0, 0, 1))


def other_core(part):
    return lax.ppermute(part, "dp", [(i, i ^ 1) for i in range(4)])


def other_chip(part):
    return lax.ppermute(part, "dp", [(i, i ^ 2) for i in range(4)])


def relocate(partner, w_gate, w_up, w_down):
    experts = partner.shape[0]
    width, hidden_units = w_gate.shape[1:]
    piece = width // experts
    stacked = jnp.stack(
        [w.reshape(experts, piece, hidden_units) for w in (w_gate, w_up, w_down)], axis=1
    )
    spread = lax.all_to_all(stacked, "expert", split_axis=0, concat_axis=0, tiled=True)
    routed = spread.at[partner].get(mode="promise_in_bounds")
    back = lax.all_to_all(routed, "expert", split_axis=0, concat_axis=0, tiled=True)
    return tuple(back[:, i].reshape(1, width, hidden_units) for i in range(3))


def dispatch(buffer):
    got = [buffer[0]] + [along_z(buffer[k], k) for k in range(1, NZ)]
    by_x = []
    for j in range(NX):
        message = jnp.stack([g[j] for g in got])
        by_x.append(message if j == 0 else along_x(message, j))
    every = jnp.stack(by_x)
    return every[:, :, 0], along_y(every[:, :, 1])


def give_back(own, other):
    every = jnp.stack([own, along_y(other)], axis=2)
    by_x = [every[0]] + [along_x(every[j], -j) for j in range(1, NX)]
    got = []
    for k in range(NZ):
        message = jnp.stack([b[k] for b in by_x])
        got.append(message if k == 0 else along_z(message, -k))
    return jnp.stack(got)


def ffn(rows, w_gate, w_up, w_down):
    gate = jnp.dot(rows, w_gate, preferred_element_type=jnp.float32)
    upper = jnp.dot(rows, w_up, preferred_element_type=jnp.float32)
    inner = (jax.nn.silu(gate) * upper).astype(jnp.bfloat16)
    return lax.dot_general(
        inner, w_down, (((1,), (1,)), ((), ())), preferred_element_type=jnp.float32
    )


def local(hidden, expert_ids, router_scores, partner, w_gate, w_up, w_down):
    rows_here, width = hidden.shape
    half = width // 2
    place = lax.axis_index("expert")
    z, x, y = place // (NX * NY), (place // NY) % NX, place % NY
    core = lax.axis_index("dp") % 2
    first = core == 0
    moved = relocate(partner, w_gate, w_up, w_down)

    row_weights = router_scores / jnp.sum(router_scores, axis=1, keepdims=True)
    facts = jnp.concatenate([expert_ids.astype(jnp.float32), row_weights], axis=1)
    facts_other = other_core(facts)
    low, high = hidden[:, :half], hidden[:, half:]
    mine = jnp.where(first, low, high)
    theirs = other_core(jnp.where(first, high, low))

    def in_order(a, b):
        return jnp.where(first, jnp.concatenate([a, b]), jnp.concatenate([b, a]))

    facts = in_order(facts, facts_other)
    rows = in_order(mine, theirs)
    choose = expert_ids.shape[1]
    ids = facts[:, :choose].astype(jnp.int32)
    weights = facts[:, choose:]
    relative = (
        ((ids // (NX * NY) - z) % NZ) * (NX * NY)
        + (((ids // NY) % NX - x) % NX) * NY
        + (ids % NY + y) % NY
    )
    experts = NZ * NX * NY
    hits = relative[:, :, None] == jnp.arange(experts, dtype=jnp.int32)
    named = jnp.any(hits, axis=1)
    row_weight = jnp.sum(jnp.where(hits, weights[:, :, None], jnp.float32(0.0)), axis=1)
    count = 2 * rows_here
    before = jnp.tril(jnp.ones((count, count), jnp.bfloat16), -1)
    rank = jnp.dot(before, named.astype(jnp.bfloat16), preferred_element_type=jnp.float32)
    taken = jnp.logical_and(
        named[:, :, None], rank[:, :, None] == jnp.arange(SLOTS, dtype=jnp.float32)
    )
    combining = jnp.where(taken, row_weight[:, :, None], jnp.float32(0.0)).reshape(count, -1)
    placing = taken.astype(jnp.bfloat16).reshape(count, -1)
    buffer = lax.dot_general(
        placing, rows, (((0,), (0,)), ((), ())), preferred_element_type=jnp.float32
    )
    buffer = buffer.astype(jnp.bfloat16).reshape(NZ, NX, NY, SLOTS, half)

    own, other = dispatch(buffer)
    here = jnp.concatenate([own.reshape(-1, half), other.reshape(-1, half)])
    both = jnp.concatenate([here, other_chip(here)])
    both_other = other_core(both)
    features = jnp.where(
        first,
        jnp.concatenate([both, both_other], axis=1),
        jnp.concatenate([both_other, both], axis=1),
    )
    output = ffn(features, w_gate[0], w_up[0], w_down[0])
    keep = jnp.where(first, output[:, :half], output[:, half:])
    send = jnp.where(first, output[:, half:], output[:, :half]).astype(jnp.bfloat16)
    summed = keep + other_core(send).astype(jnp.float32)
    block = here.shape[0]
    total = summed[:block] + other_chip(summed[block:].astype(jnp.bfloat16)).astype(jnp.float32)
    total = total.astype(jnp.bfloat16).reshape(2, NX, NZ, SLOTS, half)
    returned = give_back(total[0], total[1]).reshape(-1, half)
    mixed = jnp.dot(
        combining,
        returned.astype(jnp.float32),
        precision=lax.Precision.HIGHEST,
        preferred_element_type=jnp.float32,
    ).astype(jnp.bfloat16)
    mine = jnp.where(first, mixed[:rows_here], mixed[rows_here:])
    theirs = other_core(jnp.where(first, mixed[rows_here:], mixed[:rows_here]))
    mixed = jnp.where(
        first,
        jnp.concatenate([mine, theirs], axis=1),
        jnp.concatenate([theirs, mine], axis=1),
    )
    return (mixed,) + moved


def solution(mesh):
    rows = P(("dp", "expert"), None)
    weights = P("expert", None, "dp")
    return jax.shard_map(
        local,
        mesh=mesh,
        in_specs=(rows, rows, rows, P(), weights, weights, weights),
        out_specs=(rows, weights, weights, weights),
        check_vma=False,
    )
```

time: 663 us -> 487 us (0.73); the launches traced: 654 us -> 487 us
  waiting for transfers between devices: 117 us -> 316 us
  other arithmetic: 217 us -> 24.5 us
  local copies, waits for them, and re-layouts: 148 us -> 20.3 us
  blocking collectives: 95 us -> 0 us
  starting transfers between devices: 54.2 us -> 91.1 us
  matrix products: 20.9 us -> 33.4 us
    ppermute x0 -> x21, waiting for transfers between devices: none -> 316 us  [the longest x2 138 us: other_chip(): return lax.ppermute(part, 'dp', [(i, i ^ 2) for i in range(4)])]
    unnamed x3 -> x0, other arithmetic: 204 us -> none
    all_to_all x6 -> x2, waiting for transfers between devices: 117 us -> 0.01 us  [the longest x1 0.01 us: relocate(): lax.all_to_all(routed, 'expert', split_axis=0, concat_axis=0, tiled=True)]
    unnamed x31 -> x25, local copies, waits for them, and re-layouts: 109 us -> 1.91 us
    all_to_all x2 -> x0, blocking collectives: 95 us -> none  [local(): lax.all_to_all(shortened(routed), 'expert', split_axis=0, concat_axis=1,...]
    ppermute x0 -> x21, starting transfers between devices: none -> 66.3 us  [the longest x2 28.6 us: along_y(): return lax.ppermute(part, 'expert', expert_perm(0, 0, 1))]
    all_to_all x6 -> x2, starting transfers between devices: 54.2 us -> 24.8 us  [the longest x1 18.2 us: relocate(): lax.all_to_all(routed, 'expert', split_axis=0, concat_axis=0, tiled=True)]
    reshape x2 -> x0, local copies, waits for them, and re-layouts: 14.1 us -> none  [the longest x1 7.2 us: expert_rows(): return output.astype(jnp.bfloat16).reshape(shape)]
  transfers between devices with their start and end apart: 6 -> 23, of which waited for: 3 -> 13; matrix products, arithmetic and copies ran while one was open for 40% -> 14% of each run, Pallas kernels for 0% -> 0%
where the time goes in v1:
time: 487 us
  waiting for transfers between devices  316 us (65%)
  starting transfers between devices  91.1 us (19%)
  matrix products  33.4 us (7%)
  other arithmetic  24.5 us (5%)
  local copies, waits for them, and re-layouts  20.3 us (4%)
    ppermute x2, waiting for transfers between devices, other_chip(): return lax.ppermute(part, 'dp', [(i, i ^ 2) for i in range(4)])  138 us
    ppermute x2, waiting for transfers between devices, along_y(): return lax.ppermute(part, 'expert', expert_perm(0, 0, 1))  135 us
    dot_general x1, matrix products, ffn(): lax.dot_general(inner, w_down, (((1,), (1,)), ((), ())), preferred_elemen...  29.7 us
    ppermute x2, starting transfers between devices, along_y(): return lax.ppermute(part, 'expert', expert_perm(0, 0, 1))  28.6 us
    ppermute x6, waiting for transfers between devices, along_z(): return lax.ppermute(part, 'expert', expert_perm(step, 0, 0))  24.4 us
    ppermute x6, starting transfers between devices, along_x(): return lax.ppermute(part, 'expert', expert_perm(0, step, 0))  18.5 us
    all_to_all x1, starting transfers between devices, relocate(): lax.all_to_all(routed, 'expert', split_axis=0, concat_axis=0, tiled=True)  18.2 us
    ppermute x6, waiting for transfers between devices, along_x(): return lax.ppermute(part, 'expert', expert_perm(0, step, 0))  14.2 us
  transfers between devices with their start and end apart: 23, of which 13 were waited for; matrix products, arithmetic and copies ran while one was open for 14% of the time, Pallas kernels for 0%

profile of v1, /device:TPU:1, one launch (start us, length us, event | category | flops | bytes accessed | tf_op | source)
XLA Modules:
  0.0 486.7 jit_solution(1717267895150417289)
XLA Ops:
  0.6 0.9 reduce_sum.18
  1.5 0.8 broadcast_divide_fusion
  2.3 0.7 convert_element_type.31
  3.0 1.4 collective-permute-start
  4.4 0.9 broadcast_select_fusion.3
  5.3 0.1 collective-permute-start.1
  5.8 0.5 copy-done.8
  6.3 0.1 fusion.22
  6.4 0.2 fusion.42
  6.6 0.1 copy.29
  6.7 0.5 convolution_convert_fusion
  7.3 1.8 collective-permute-start.2
  9.1 3.3 collective-permute-start.3
  12.4 0.7 collective-permute-start.4
  13.1 4.4 collective-permute-done.2
  17.5 6.5 %collective-permute-done.3 = bf16[4,2,8,2048]{3,2,1,0:T(8,128)(2,1)S(1)} collective-permute-done((bf16[4,2,8,2048]{3,2,1,0:T(8,128)(2,1)S(1)}, bf16[4,2,8,2048]{3,2,1,0:T(8,128)(2,1)S(1)}, u32[]{:S(2)}, u32[]{:S(2)}) %collective-permute-start.3) | collective-permute-done | bytes 262176 | tf_op jit(solution)/shard_map/ppermute | solution.py:20
  23.9 0.6 fusion.73
  24.6 0.6 fusion.74
  25.3 1.3 collective-permute-start.5
  26.6 0.7 pad_maximum_fusion.6
  27.3 2.4 collective-permute-start.6
  29.8 0.7 pad_maximum_fusion.7
  30.5 1.2 collective-permute-start.7
  31.7 7.0 %pad_maximum_fusion = bf16[32,3,128,384]{3,2,1,0:T(8,128)(2,1)} fusion(bf16[32,1,128,384]{3,2,1,0:T(8,128)(2,1)} %bitcast.94, bf16[32,1,128,384]{3,2,1,0:T(8,128)(2,1)S(1)} %bitcast.93, bf16[32,1,128,384]{3,2,1,0:T(8,128)(2,1)} %bitcast.95), kind=kLoop, calls=%fused_computation.1 | loop fusion | flops 9437184 | bytes 18874368 | tf_op jit(solution)/shard_map/stack | solution.py:43
  38.7 6.6 %all-to-all-start = ((bf16[32,3,128,384]{3,2,1,0:T(8,128)(2,1)}), bf16[32,3,128,384]{3,2,1,0:T(8,128)(2,1)}, u32[]{:S(2)}, u32[]{:S(2)}) async-start(bf16[32,3,128,384]{3,2,1,0:T(8,128)(2,1)} %pad_maximum_fusion), calls=%async_computation | async-start | bytes 18874368 | tf_op jit(solution)/shard_map/all_to_all | solution.py:46
  45.4 1.2 pad_maximum_fusion.2
  46.7 0.1 fusion.67
  46.8 2.7 collective-permute-start.8
  49.5 123.8 %collective-permute-done.8 = bf16[4,4,8,2048]{3,2,1,0:T(8,128)(2,1)S(1)} collective-permute-done((bf16[4,4,8,2048]{3,2,1,0:T(8,128)(2,1)S(1)}, bf16[4,4,8,2048]{3,2,1,0:T(8,128)(2,1)S(1)}, u32[]{:S(2)}, u32[]{:S(2)}) %collective-permute-start.8) | collective-permute-done | bytes 524320 | tf_op jit(solution)/shard_map/ppermute | solution.py:28
  173.4 1.5 collective-permute-start.9
  174.9 20.9 %collective-permute-done.9 = bf16[256,2048]{1,0:T(8,128)(2,1)S(1)} collective-permute-done((bf16[256,2048]{1,0:T(8,128)(2,1)S(1)}, bf16[256,2048]{1,0:T(8,128)(2,1)S(1)}, u32[]{:S(2)}, u32[]{:S(2)}) %collective-permute-start.9) | collective-permute-done | bytes 1048608 | tf_op jit(solution)/shard_map/ppermute | solution.py:36
  195.8 0.1 pad_maximum_fusion.1
  196.0 3.3 collective-permute-start.10
  199.2 3.8 collective-permute-done.10
  203.0 1.3 copy-done.9
  204.4 2.4 fusion.2
  206.7 29.7 %fusion = f32[512,4096]{1,0:T(8,128)} fusion(bf16[1,4096,384]{2,1,0:T(8,128)(2,1)} %param.13, f32[512,384]{1,0:T(8,128)S(1)} %fusion.2, bf16[1,4096,384]{2,1,0:T(8,128)(2,1)} %param.11, bf16[512,2048]{1,0:T(8,128)(2,1)} %copy-done.9, bf16[256,2048]{1,0:T(8,128)(2,1)S(1)} %collective-permute-done.9, bf16[128,2048]{1,0:T(8,128)(2,1)S(1)} %bitcast.104, ...), kind=kOutput, calls=%fused_computation.5 | convolution fusion | flops 3258056704 | bytes 19660800 | tf_op jit(solution)/shard_map/dot_general | solution.py:76
  236.5 3.8 select_convert_fusion
  240.3 0.5 collective-permute-start.11
  240.8 9.6 %gather_fusion = bf16[32,3,128,384]{3,2,1,0:T(8,128)(2,1)} fusion(bf16[32,3,128,384]{3,2,1,0:T(8,128)(2,1)} %all-to-all-done, s32[1024]{0:T(1024)S(1)} %pad_clamp_fusion), kind=kCustom, calls=%fused_computation | custom fusion | bytes 18874496 | tf_op jit(solution)/shard_map/gather | solution.py:47
  250.4 18.2 %all-to-all-start.1 = ((bf16[32,3,128,384]{3,2,1,0:T(8,128)(2,1)}), bf16[32,3,128,384]{3,2,1,0:T(8,128)(2,1)}, u32[]{:S(2)}, u32[]{:S(2)}) async-start(bf16[32,3,128,384]{3,2,1,0:T(8,128)(2,1)} %gather_fusion), calls=%async_computation.1 | async-start | bytes 18874368 | tf_op jit(solution)/shard_map/all_to_all | solution.py:48
  268.6 5.6 %convert_add_fusion = f32[512,2048]{1,0:T(8,128)S(1)} fusion(bf16[512,2048]{1,0:T(8,128)(2,1)} %collective-permute-done.11, f32[512,4096]{1,0:T(8,128)} %fusion, pred[]{:T(512)S(6)} %eq.58), kind=kLoop, calls=%fused_computation.3 | loop fusion | flops 3145728 | bytes 14680065 | tf_op jit(solution)/shard_map/add | solution.py:139
  274.2 0.1 slice.393
  274.3 1.5 collective-permute-start.12
  275.9 117.4 %collective-permute-done.12 = bf16[256,2048]{1,0:T(8,128)(2,1)S(1)} collective-permute-done((bf16[256,2048]{1,0:T(8,128)(2,1)S(1)}, bf16[256,2048]{1,0:T(8,128)(2,1)S(1)}, u32[]{:S(2)}, u32[]{:S(2)}) %collective-permute-start.12) | collective-permute-done | bytes 1048608 | tf_op jit(solution)/shard_map/ppermute | solution.py:36
  393.3 0.3 fusion.6
  393.7 25.8 %collective-permute-start.13 = (bf16[4,4,8,2048]{3,2,1,0:T(8,128)(2,1)S(1)}, bf16[4,4,8,2048]{3,2,1,0:T(8,128)(2,1)S(1)}, u32[]{:S(2)}, u32[]{:S(2)}) collective-permute-start(bf16[4,4,8,2048]{3,2,1,0:T(8,128)(2,1)S(1)} %bitcast.105), channel_id=1, source_target_pairs={{0,1},{1,0},{2,3},{3,2},{4,5},{5,4},{6,7},{7,6},{8,9},{9,8},{10,11... | collective-permute-start | bytes 1572872 | tf_op jit(solution)/shard_map/ppermute | solution.py:28
  419.5 11.0 %collective-permute-done.13 = bf16[4,4,8,2048]{3,2,1,0:T(8,128)(2,1)S(1)} collective-permute-done((bf16[4,4,8,2048]{3,2,1,0:T(8,128)(2,1)S(1)}, bf16[4,4,8,2048]{3,2,1,0:T(8,128)(2,1)S(1)}, u32[]{:S(2)}, u32[]{:S(2)}) %collective-permute-start.13) | collective-permute-done | bytes 524320 | tf_op jit(solution)/shard_map/ppermute | solution.py:28
  430.6 12.9 %collective-permute-start.14 = (bf16[4,2,8,2048]{3,2,1,0:T(8,128)(2,1)S(1)}, bf16[4,2,8,2048]{3,2,1,0:T(8,128)(2,1)S(1)}, u32[]{:S(2)}, u32[]{:S(2)}) collective-permute-start(bf16[4,2,8,2048]{3,2,1,0:T(8,128)(2,1)S(1)} %bitcast.107), channel_id=1, source_target_pairs={{0,6},{1,7},{2,0},{3,1},{4,2},{5,3},{6,4},{7,5},{8,14},{9,15},{10,... | collective-permute-start | bytes 786440 | tf_op jit(solution)/shard_map/ppermute | solution.py:24
  443.7 0.6 collective-permute-start.16
  444.4 10.2 %collective-permute-done.14 = bf16[4,2,8,2048]{3,2,1,0:T(8,128)(2,1)S(1)} collective-permute-done((bf16[4,2,8,2048]{3,2,1,0:T(8,128)(2,1)S(1)}, bf16[4,2,8,2048]{3,2,1,0:T(8,128)(2,1)S(1)}, u32[]{:S(2)}, u32[]{:S(2)}) %collective-permute-start.14) | collective-permute-done | bytes 262176 | tf_op jit(solution)/shard_map/ppermute | solution.py:24
  454.7 4.0 collective-permute-done.16
  458.7 2.9 collective-permute-start.17
  461.7 1.5 collective-permute-start.18
  463.3 0.1 select_reduce_fusion
  463.6 3.7 collective-permute-done.17
  467.3 2.9 collective-permute-done.18
  470.2 7.0 %collective-permute-done.19 = bf16[4,2,8,2048]{3,2,1,0:T(8,128)(2,1)S(1)} collective-permute-done((bf16[4,2,8,2048]{3,2,1,0:T(8,128)(2,1)S(1)}, bf16[4,2,8,2048]{3,2,1,0:T(8,128)(2,1)S(1)}, u32[]{:S(2)}, u32[]{:S(2)}) %collective-permute-start.19) | collective-permute-done | bytes 262176 | tf_op jit(solution)/shard_map/ppermute | solution.py:20
  477.1 0.1 pad_maximum_fusion.4
  477.3 0.7 convolution_convert_fusion.1
  478.0 0.6 collective-permute-start.20
  478.6 0.9 collective-permute-done.20
  479.5 0.7 maximum_select_fusion.3
  480.2 6.6 %fusion.65 = (bf16[32,1,128,384]{3,2,1,0:T(8,128)(2,1)}, bf16[32,1,128,384]{3,2,1,0:T(8,128)(2,1)}, bf16[32,1,128,384]{3,2,1,0:T(8,128)(2,1)}) fusion(bf16[32,3,128,384]{3,2,1,0:T(8,128)(2,1)} %all-to-all-done.1), kind=kLoop, calls=%fused_computation.139 | loop fusion | bytes 18874368 | tf_op jit(solution)/shard_map/slice | solution.py:49
  (65 shorter events, 1.4 us)
Async XLA Ops:
  0.6 31.0 %copy-start = (bf16[1,4096,384]{2,1,0:T(8,128)(2,1)S(1)}, bf16[1,4096,384]{2,1,0:T(8,128)(2,1)}, u32[]{:S(2)}) copy-start(bf16[1,4096,384]{2,1,0:T(8,128)(2,1)} %param.12) | copy-start | bytes 9437188
  3.0 2.6 collective-permute-start
  5.3 1.4 collective-permute-start.1
  5.7 0.6 copy-start.8
  6.6 18.7 %copy-start.4 = (f32[32,32]{0,1:T(8,128)}, f32[32,32]{0,1:T(8,128)S(1)}, u32[]{:S(2)}) copy-start(f32[32,32]{0,1:T(8,128)S(1)} %fusion.42) | copy-start | bytes 12292
  6.7 18.6 %copy-start.6 = (pred[32,32]{0,1:T(8,128)(4,1)}, pred[32,32]{0,1:T(8,128)(4,1)S(1)}, u32[]{:S(2)}) copy-start(pred[32,32]{0,1:T(8,128)(4,1)S(1)} %copy.29) | copy-start | bytes 3076
  7.3 10.2 %collective-permute-start.2 = (bf16[4,2,8,2048]{3,2,1,0:T(8,128)(2,1)S(1)}, bf16[4,2,8,2048]{3,2,1,0:T(8,128)(2,1)S(1)}, u32[]{:S(2)}, u32[]{:S(2)}) collective-permute-start(bf16[4,2,8,2048]{3,2,1,0:T(8,128)(2,1)S(1)} %bitcast.111), channel_id=1, source_target_pairs={{0,8},{1,9},{2,10},{3,11},{4,12},{5,13},{6,14},{7,15},{8,16},{9,17... | collective-permute-start | bytes 786440 | tf_op jit(solution)/shard_map/ppermute | solution.py:20
  9.1 14.9 %collective-permute-start.3 = (bf16[4,2,8,2048]{3,2,1,0:T(8,128)(2,1)S(1)}, bf16[4,2,8,2048]{3,2,1,0:T(8,128)(2,1)S(1)}, u32[]{:S(2)}, u32[]{:S(2)}) collective-permute-start(bf16[4,2,8,2048]{3,2,1,0:T(8,128)(2,1)S(1)} %bitcast.110), channel_id=1, source_target_pairs={{0,16},{1,17},{2,18},{3,19},{4,20},{5,21},{6,22},{7,23},{8,24},{9,... | collective-permute-start | bytes 786440 | tf_op jit(solution)/shard_map/ppermute | solution.py:20
  12.4 12.2 %collective-permute-start.4 = (bf16[4,2,8,2048]{3,2,1,0:T(8,128)(2,1)S(1)}, bf16[4,2,8,2048]{3,2,1,0:T(8,128)(2,1)S(1)}, u32[]{:S(2)}, u32[]{:S(2)}) collective-permute-start(bf16[4,2,8,2048]{3,2,1,0:T(8,128)(2,1)S(1)} %bitcast.109), channel_id=1, source_target_pairs={{0,24},{1,25},{2,26},{3,27},{4,28},{5,29},{6,30},{7,31},{8,0},{9,1... | collective-permute-start | bytes 786440 | tf_op jit(solution)/shard_map/ppermute | solution.py:20
  25.3 20.1 %collective-permute-start.5 = (bf16[4,2,8,2048]{3,2,1,0:T(8,128)(2,1)S(1)}, bf16[4,2,8,2048]{3,2,1,0:T(8,128)(2,1)}, u32[]{:S(2)}, u32[]{:S(2)}) collective-permute-start(bf16[4,2,8,2048]{3,2,1,0:T(8,128)(2,1)S(1)} %pad_maximum_fusion.5), channel_id=1, source_target_pairs={{0,2},{1,3},{2,4},{3,5},{4,6},{5,7},{6,0},{7,1},{8,10},{9,11},{10,... | collective-permute-start | bytes 786440 | tf_op jit(solution)/shard_map/ppermute | solution.py:24
  27.3 18.1 %collective-permute-start.6 = (bf16[4,2,8,2048]{3,2,1,0:T(8,128)(2,1)}, bf16[4,2,8,2048]{3,2,1,0:T(8,128)(2,1)}, u32[]{:S(2)}, u32[]{:S(2)}) collective-permute-start(bf16[4,2,8,2048]{3,2,1,0:T(8,128)(2,1)} %pad_maximum_fusion.6), channel_id=1, source_target_pairs={{0,4},{1,5},{2,6},{3,7},{4,0},{5,1},{6,2},{7,3},{8,12},{9,13},{10,... | collective-permute-start | bytes 786440 | tf_op jit(solution)/shard_map/ppermute | solution.py:24
  30.5 14.9 %collective-permute-start.7 = (bf16[4,2,8,2048]{3,2,1,0:T(8,128)(2,1)}, bf16[4,2,8,2048]{3,2,1,0:T(8,128)(2,1)}, u32[]{:S(2)}, u32[]{:S(2)}) collective-permute-start(bf16[4,2,8,2048]{3,2,1,0:T(8,128)(2,1)} %pad_maximum_fusion.7), channel_id=1, source_target_pairs={{0,6},{1,7},{2,0},{3,1},{4,2},{5,3},{6,4},{7,5},{8,14},{9,15},{10,... | collective-permute-start | bytes 786440 | tf_op jit(solution)/shard_map/ppermute | solution.py:24
  38.7 6.6 %copy-start.2 = (bf16[1,2,8,2048]{3,2,1,0:T(8,128)(2,1)S(1)}, bf16[1,2,8,2048]{3,2,1,0:T(8,128)(2,1)}, u32[]{:S(2)}) copy-start(bf16[1,2,8,2048]{3,2,1,0:T(8,128)(2,1)} %get-tuple-element.41) | copy-start | bytes 196612
  38.7 6.6 %copy-start.3 = (bf16[1,2,8,2048]{3,2,1,0:T(8,128)(2,1)S(1)}, bf16[1,2,8,2048]{3,2,1,0:T(8,128)(2,1)}, u32[]{:S(2)}) copy-start(bf16[1,2,8,2048]{3,2,1,0:T(8,128)(2,1)} %get-tuple-element.45) | copy-start | bytes 196612
  38.7 202.1 %all-to-all-start = ((bf16[32,3,128,384]{3,2,1,0:T(8,128)(2,1)}), bf16[32,3,128,384]{3,2,1,0:T(8,128)(2,1)}, u32[]{:S(2)}, u32[]{:S(2)}) async-start(bf16[32,3,128,384]{3,2,1,0:T(8,128)(2,1)} %pad_maximum_fusion), calls=%async_computation | async-start | bytes 18874368 | tf_op jit(solution)/shard_map/all_to_all | solution.py:46
  46.6 157.7 %copy-start.1 = (bf16[1,4096,384]{2,1,0:T(8,128)(2,1)S(1)}, bf16[1,4096,384]{2,1,0:T(8,128)(2,1)}, u32[]{:S(2)}) copy-start(bf16[1,4096,384]{2,1,0:T(8,128)(2,1)} %param.12) | copy-start | bytes 9437188
  46.8 126.5 %collective-permute-start.8 = (bf16[4,4,8,2048]{3,2,1,0:T(8,128)(2,1)S(1)}, bf16[4,4,8,2048]{3,2,1,0:T(8,128)(2,1)S(1)}, u32[]{:S(2)}, u32[]{:S(2)}) collective-permute-start(bf16[4,4,8,2048]{3,2,1,0:T(8,128)(2,1)S(1)} %get-tuple-element.17), channel_id=1, source_target_pairs={{0,1},{1,0},{2,3},{3,2},{4,5},{5,4},{6,7},{7,6},{8,9},{9,8},{10,11... | collective-permute-start | bytes 1572872 | tf_op jit(solution)/shard_map/ppermute | solution.py:28
  173.4 22.5 %collective-permute-start.9 = (bf16[256,2048]{1,0:T(8,128)(2,1)S(1)}, bf16[256,2048]{1,0:T(8,128)(2,1)S(1)}, u32[]{:S(2)}, u32[]{:S(2)}) collective-permute-start(bf16[256,2048]{1,0:T(8,128)(2,1)S(1)} %pad_maximum_fusion.3), channel_id=1, source_target_pairs={{0,64},{32,96},{64,0},{96,32},{1,65},{33,97},{65,1},{97,33},{2,66}... | collective-permute-start | bytes 3145736 | tf_op jit(solution)/shard_map/ppermute | solution.py:36
  196.0 7.1 %collective-permute-start.10 = (bf16[512,2048]{1,0:T(8,128)(2,1)S(1)}, bf16[512,2048]{1,0:T(8,128)(2,1)S(1)}, u32[]{:S(2)}, u32[]{:S(2)}) collective-permute-start(bf16[512,2048]{1,0:T(8,128)(2,1)S(1)} %pad_maximum_fusion.1), channel_id=1, source_target_pairs={{0,32},{32,0},{64,96},{96,64},{1,33},{33,1},{65,97},{97,65},{2,34}... | collective-permute-start | bytes 6291464 | tf_op jit(solution)/shard_map/ppermute | solution.py:32
  203.0 1.3 copy-start.9
  236.4 4.3 copy-start.10
  240.3 28.3 %collective-permute-start.11 = (bf16[512,2048]{1,0:T(8,128)(2,1)S(1)}, bf16[512,2048]{1,0:T(8,128)(2,1)}, u32[]{:S(2)}, u32[]{:S(2)}) collective-permute-start(bf16[512,2048]{1,0:T(8,128)(2,1)S(1)} %select_convert_fusion), channel_id=1, source_target_pairs={{0,32},{32,0},{64,96},{96,64},{1,33},{33,1},{65,97},{97,65},{2,34}... | collective-permute-start | bytes 6291464 | tf_op jit(solution)/shard_map/ppermute | solution.py:32
  250.4 229.8 %all-to-all-start.1 = ((bf16[32,3,128,384]{3,2,1,0:T(8,128)(2,1)}), bf16[32,3,128,384]{3,2,1,0:T(8,128)(2,1)}, u32[]{:S(2)}, u32[]{:S(2)}) async-start(bf16[32,3,128,384]{3,2,1,0:T(8,128)(2,1)} %gather_fusion), calls=%async_computation.1 | async-start | bytes 18874368 | tf_op jit(solution)/shard_map/all_to_all | solution.py:48
  274.3 169.2 %slice-start = ((f32[32,16]{0,1:T(8,128)}), f32[32,8]{0,1:T(8,128)S(1)}, s32[]{:S(2)}) async-start(f32[32,16]{0,1:T(8,128)} %copy-done.8), calls=%async_computation.2 | async-start | bytes 8192 | tf_op jit(solution)/shard_map/slice | solution.py:104
  274.3 118.9 %collective-permute-start.12 = (bf16[256,2048]{1,0:T(8,128)(2,1)S(1)}, bf16[256,2048]{1,0:T(8,128)(2,1)S(1)}, u32[]{:S(2)}, u32[]{:S(2)}) collective-permute-start(bf16[256,2048]{1,0:T(8,128)(2,1)S(1)} %slice.393), channel_id=1, source_target_pairs={{0,64},{32,96},{64,0},{96,32},{1,65},{33,97},{65,1},{97,33},{2,66}... | collective-permute-start | bytes 3145736 | tf_op jit(solution)/shard_map/ppermute | solution.py:36
  393.7 36.8 %collective-permute-start.13 = (bf16[4,4,8,2048]{3,2,1,0:T(8,128)(2,1)S(1)}, bf16[4,4,8,2048]{3,2,1,0:T(8,128)(2,1)S(1)}, u32[]{:S(2)}, u32[]{:S(2)}) collective-permute-start(bf16[4,4,8,2048]{3,2,1,0:T(8,128)(2,1)S(1)} %bitcast.105), channel_id=1, source_target_pairs={{0,1},{1,0},{2,3},{3,2},{4,5},{5,4},{6,7},{7,6},{8,9},{9,8},{10,11... | collective-permute-start | bytes 1572872 | tf_op jit(solution)/shard_map/ppermute | solution.py:28
  430.6 46.7 %copy-start.5 = (f32[32,32]{0,1:T(8,128)S(1)}, f32[32,32]{0,1:T(8,128)}, u32[]{:S(2)}) copy-start(f32[32,32]{0,1:T(8,128)} %copy-done.4) | copy-start | bytes 12292
  430.6 46.7 %copy-start.7 = (pred[32,32]{0,1:T(8,128)(4,1)S(1)}, pred[32,32]{0,1:T(8,128)(4,1)}, u32[]{:S(2)}) copy-start(pred[32,32]{0,1:T(8,128)(4,1)} %copy-done.6) | copy-start | bytes 3076
  430.6 24.0 %collective-permute-start.14 = (bf16[4,2,8,2048]{3,2,1,0:T(8,128)(2,1)S(1)}, bf16[4,2,8,2048]{3,2,1,0:T(8,128)(2,1)S(1)}, u32[]{:S(2)}, u32[]{:S(2)}) collective-permute-start(bf16[4,2,8,2048]{3,2,1,0:T(8,128)(2,1)S(1)} %bitcast.107), channel_id=1, source_target_pairs={{0,6},{1,7},{2,0},{3,1},{4,2},{5,3},{6,4},{7,5},{8,14},{9,15},{10,... | collective-permute-start | bytes 786440 | tf_op jit(solution)/shard_map/ppermute | solution.py:24
  443.6 11.0 %collective-permute-start.15 = (bf16[4,2,8,2048]{3,2,1,0:T(8,128)(2,1)S(1)}, bf16[4,2,8,2048]{3,2,1,0:T(8,128)(2,1)S(1)}, u32[]{:S(2)}, u32[]{:S(2)}) collective-permute-start(bf16[4,2,8,2048]{3,2,1,0:T(8,128)(2,1)S(1)} %bitcast.108), channel_id=1, source_target_pairs={{0,4},{1,5},{2,6},{3,7},{4,0},{5,1},{6,2},{7,3},{8,12},{9,13},{10,... | collective-permute-start | bytes 786440 | tf_op jit(solution)/shard_map/ppermute | solution.py:24
  443.7 14.9 %collective-permute-start.16 = (bf16[4,2,8,2048]{3,2,1,0:T(8,128)(2,1)S(1)}, bf16[4,2,8,2048]{3,2,1,0:T(8,128)(2,1)S(1)}, u32[]{:S(2)}, u32[]{:S(2)}) collective-permute-start(bf16[4,2,8,2048]{3,2,1,0:T(8,128)(2,1)S(1)} %bitcast.106), channel_id=1, source_target_pairs={{0,2},{1,3},{2,4},{3,5},{4,6},{5,7},{6,0},{7,1},{8,10},{9,11},{10,... | collective-permute-start | bytes 786440 | tf_op jit(solution)/shard_map/ppermute | solution.py:24
  458.7 8.6 %collective-permute-start.17 = (bf16[4,2,8,2048]{3,2,1,0:T(8,128)(2,1)S(1)}, bf16[4,2,8,2048]{3,2,1,0:T(8,128)(2,1)S(1)}, u32[]{:S(2)}, u32[]{:S(2)}) collective-permute-start(bf16[4,2,8,2048]{3,2,1,0:T(8,128)(2,1)S(1)} %pad_maximum_fusion.8), channel_id=1, source_target_pairs={{0,24},{1,25},{2,26},{3,27},{4,28},{5,29},{6,30},{7,31},{8,0},{9,1... | collective-permute-start | bytes 786440 | tf_op jit(solution)/shard_map/ppermute | solution.py:20
  461.7 8.5 %collective-permute-start.18 = (bf16[4,2,8,2048]{3,2,1,0:T(8,128)(2,1)S(1)}, bf16[4,2,8,2048]{3,2,1,0:T(8,128)(2,1)S(1)}, u32[]{:S(2)}, u32[]{:S(2)}) collective-permute-start(bf16[4,2,8,2048]{3,2,1,0:T(8,128)(2,1)S(1)} %pad_maximum_fusion.9), channel_id=1, source_target_pairs={{0,16},{1,17},{2,18},{3,19},{4,20},{5,21},{6,22},{7,23},{8,24},{9,... | collective-permute-start | bytes 786440 | tf_op jit(solution)/shard_map/ppermute | solution.py:20
  463.2 13.9 %collective-permute-start.19 = (bf16[4,2,8,2048]{3,2,1,0:T(8,128)(2,1)S(1)}, bf16[4,2,8,2048]{3,2,1,0:T(8,128)(2,1)S(1)}, u32[]{:S(2)}, u32[]{:S(2)}) collective-permute-start(bf16[4,2,8,2048]{3,2,1,0:T(8,128)(2,1)S(1)} %pad_maximum_fusion.10), channel_id=1, source_target_pairs={{0,8},{1,9},{2,10},{3,11},{4,12},{5,13},{6,14},{7,15},{8,16},{9,17... | collective-permute-start | bytes 786440 | tf_op jit(solution)/shard_map/ppermute | solution.py:20
  478.0 1.5 collective-permute-start.20

commit v2 on v1

v2 whole, which is shorter than its diff:
```python
import jax
import jax.numpy as jnp
from jax import lax
from jax.experimental import pallas as pl
from jax.experimental.pallas import tpu as pltpu
from jax.sharding import PartitionSpec as P

EXPERTS = 32
SLOTS = 8
LANES = 384


def other_core(part):
    return lax.ppermute(part, "dp", [(i, i ^ 1) for i in range(4)])


def exchange(part):
    return lax.all_to_all(part, "expert", split_axis=0, concat_axis=0, tiled=True)


def pack_rows(rows):
    blocks = -(-rows.shape[1] // LANES)
    padded = jnp.pad(rows, ((0, 0), (0, blocks * LANES - rows.shape[1])))
    return [
        padded[:, b * LANES : (b + 1) * LANES].reshape(EXPERTS, SLOTS, LANES)
        for b in range(blocks)
    ]


def unpack_rows(packed, half):
    blocks = packed.shape[1] // SLOTS
    pieces = [
        packed[:, b * SLOTS : (b + 1) * SLOTS].reshape(EXPERTS * SLOTS, LANES)
        for b in range(blocks)
    ]
    pieces[-1] = pieces[-1][:, : half - (blocks - 1) * LANES]
    return jnp.concatenate(pieces, axis=1)


GROUP = 4


def pick_kernel(count, partner_ref, *refs):
    out = refs[-1]
    for g in range(GROUP):
        at = 0
        for i in range(count):
            block = refs[g * count + i]
            out[g, at : at + block.shape[1], :] = block[0]
            at += block.shape[1]


def pick(partner, sources):
    piece = 128
    count = len(sources)
    specs, operands = [], []
    for g in range(GROUP):
        for array, block in sources:
            specs.append(
                pl.BlockSpec(
                    (1, piece, LANES),
                    lambda i, p, g=g, block=block: (p[i * GROUP + g], block, 0),
                )
            )
            operands.append(array)
    size = EXPERTS * count * piece * LANES * 2
    return pl.pallas_call(
        lambda *refs: pick_kernel(count, *refs),
        out_shape=jax.ShapeDtypeStruct((EXPERTS, count * piece, LANES), jnp.bfloat16),
        grid_spec=pltpu.PrefetchScalarGridSpec(
            num_scalar_prefetch=1,
            grid=(EXPERTS // GROUP,),
            in_specs=specs,
            out_specs=pl.BlockSpec((GROUP, count * piece, LANES), lambda i, p: (i, 0, 0)),
        ),
        cost_estimate=pl.CostEstimate(flops=0, bytes_accessed=2 * size, transcendentals=0),
        name="pick",
    )(partner, *operands)


def ffn_kernel(rows_ref, gate_ref, up_ref, down_ref, out_ref):
    half = rows_ref.shape[2]

    def product(w_ref):
        return jnp.dot(
            rows_ref[0], w_ref[:half, :], preferred_element_type=jnp.float32
        ) + jnp.dot(rows_ref[1], w_ref[half:, :], preferred_element_type=jnp.float32)

    gate = product(gate_ref)
    upper = product(up_ref)
    inner = (gate / (1.0 + jnp.exp(-gate)) * upper).astype(jnp.bfloat16)
    for c in range(2):
        out_ref[c] = lax.dot_general(
            inner,
            down_ref[c * half : (c + 1) * half, :],
            (((1,), (1,)), ((), ())),
            preferred_element_type=jnp.float32,
        ).astype(jnp.bfloat16)


def ffn(rows, w_gate, w_up, w_down):
    groups, count, half = rows.shape
    width, hidden_units = w_gate.shape
    whole = pl.BlockSpec((width, hidden_units), lambda i: (0, 0))
    block = pl.BlockSpec((2, count, half), lambda i: (i, 0, 0))
    flops = 2 * 3 * groups * count * half * hidden_units
    size = 2 * (2 * groups * count * half + 3 * width * hidden_units)
    return pl.pallas_call(
        ffn_kernel,
        out_shape=jax.ShapeDtypeStruct(rows.shape, jnp.bfloat16),
        grid=(groups // 2,),
        in_specs=[block, whole, whole, whole],
        out_specs=block,
        compiler_params=pltpu.CompilerParams(vmem_limit_bytes=48 * 2**20),
        cost_estimate=pl.CostEstimate(
            flops=flops, bytes_accessed=size, transcendentals=groups * count * hidden_units // 2
        ),
        name="ffn",
    )(rows, w_gate, w_up, w_down)


def local(hidden, expert_ids, router_scores, partner, w_gate, w_up, w_down):
    rows_here, width = hidden.shape
    half = width // 2
    piece = width // EXPERTS
    first = lax.axis_index("dp") % 2 == 0
    gate, upper, down = (w.reshape(EXPERTS, piece, LANES) for w in (w_gate, w_up, w_down))

    row_weights = router_scores / jnp.sum(router_scores, axis=1, keepdims=True)
    facts = jnp.concatenate([expert_ids.astype(jnp.float32), row_weights], axis=1)
    facts_other = other_core(facts)
    low, high = hidden[:, :half], hidden[:, half:]
    mine = jnp.where(first, low, high)
    theirs = other_core(jnp.where(first, high, low))

    def in_order(a, b):
        return jnp.where(first, jnp.concatenate([a, b]), jnp.concatenate([b, a]))

    facts = in_order(facts, facts_other)
    rows = in_order(mine, theirs)
    choose = expert_ids.shape[1]
    ids = facts[:, :choose].astype(jnp.int32)
    weights = facts[:, choose:]
    hits = ids[:, :, None] == jnp.arange(EXPERTS, dtype=jnp.int32)
    named = jnp.any(hits, axis=1)
    row_weight = jnp.sum(jnp.where(hits, weights[:, :, None], jnp.float32(0.0)), axis=1)
    count = 2 * rows_here
    before = jnp.tril(jnp.ones((count, count), jnp.bfloat16), -1)
    rank = jnp.dot(before, named.astype(jnp.bfloat16), preferred_element_type=jnp.float32)
    taken = jnp.logical_and(
        named[:, :, None], rank[:, :, None] == jnp.arange(SLOTS, dtype=jnp.float32)
    )
    combining = jnp.where(taken, row_weight[:, :, None], jnp.float32(0.0)).reshape(count, -1)
    placing = taken.astype(jnp.bfloat16).reshape(count, -1)
    buffer = lax.dot_general(
        placing, rows, (((0,), (0,)), ((), ())), preferred_element_type=jnp.float32
    ).astype(jnp.bfloat16)

    spread_a = exchange(jnp.concatenate([gate] + pack_rows(buffer), axis=1))
    outgoing_b = jnp.concatenate([upper, down], axis=1)
    spread_a, outgoing_b = lax.optimization_barrier((spread_a, outgoing_b))
    spread_b = exchange(outgoing_b)

    arrived = unpack_rows(spread_a[:, piece:], half)
    every = lax.all_gather(arrived, "dp", axis=0)
    output = ffn(every, w_gate[0], w_up[0], w_down[0])
    total = lax.psum_scatter(output, "dp", scatter_dimension=0)

    routed_a = pick(partner, [(spread_a, 0), (spread_b, 0)])
    back_a = exchange(routed_a)
    routed_b = jnp.concatenate([pick(partner, [(spread_b, 1)])] + pack_rows(total), axis=1)
    back_a, routed_b = lax.optimization_barrier((back_a, routed_b))
    back_b = exchange(routed_b)

    returned = unpack_rows(back_b[:, piece:], half)
    mixed = jnp.dot(
        combining,
        returned.astype(jnp.float32),
        precision=lax.Precision.HIGHEST,
        preferred_element_type=jnp.float32,
    ).astype(jnp.bfloat16)
    mine = jnp.where(first, mixed[:rows_here], mixed[rows_here:])
    theirs = other_core(jnp.where(first, mixed[rows_here:], mixed[:rows_here]))
    mixed = jnp.where(
        first,
        jnp.concatenate([mine, theirs], axis=1),
        jnp.concatenate([theirs, mine], axis=1),
    )
    moved = (back_a[:, :piece], back_a[:, piece:], back_b[:, :piece])
    return (mixed,) + tuple(m.reshape(w_gate.shape) for m in moved)


def solution(mesh):
    rows = P(("dp", "expert"), None)
    weights = P("expert", None, "dp")
    return jax.shard_map(
        local,
        mesh=mesh,
        in_specs=(rows, rows, rows, P(), weights, weights, weights),
        out_specs=(rows, weights, weights, weights),
        check_vma=False,
    )
```

time: 487 us -> 459 us (0.943)
  starting transfers between devices: 91.1 us -> 41.3 us
  matrix products: 33.4 us -> 1.43 us
  Pallas kernels: 0 us -> 27.5 us
  local copies, waits for them, and re-layouts: 20.3 us -> 46 us
  other arithmetic: 24.5 us -> 9.45 us
  between operations: 1.1 us -> 14.3 us
    ppermute x16 -> x0, waiting for transfers between devices: 312 us -> none  [the longest x2 138 us: other_chip(): return lax.ppermute(part, 'dp', [(i, i ^ 2) for i in range(4)])]
    all_to_all x2 -> x4, waiting for transfers between devices: 0.01 us -> 112 us  [exchange(): lax.all_to_all(part, 'expert', split_axis=0, concat_axis=0, tiled=True)]
    all_gather x0 -> x1, waiting for transfers between devices: none -> 110 us  [local(): every = lax.all_gather(arrived, 'dp', axis=0)]
    reduce_scatter x0 -> x1, waiting for transfers between devices: none -> 95.6 us  [local(): total = lax.psum_scatter(output, 'dp', scatter_dimension=0)]
    ppermute x16 -> x0, starting transfers between devices: 60.5 us -> none  [the longest x2 28.6 us: along_y(): return lax.ppermute(part, 'expert', expert_perm(0, 0, 1))]
    dot_general x2 -> x0, matrix products: 32.1 us -> none  [the longest x1 29.7 us: ffn(): lax.dot_general(inner, w_down, (((1,), (1,)), ((), ())), preferred_elemen...]
    unnamed x25 -> x28, local copies, waits for them, and re-layouts: 1.91 us -> 30.5 us
    pallas_call x0 -> x3, Pallas kernels: none -> 27.5 us  [the longest x2 15.6 us: pick(): pl.pallas_call(lambda *refs: pick_kernel(count, *refs), out_shape=jax.Sha...]
  transfers between devices with their start and end apart: 23 -> 9, of which waited for: 13 -> 4; matrix products, arithmetic and copies ran while one was open for 14% -> 8% of each run, Pallas kernels for 0% -> 6%
where the time goes in v2:
time: 459 us; the launch traced here: 457 us
  waiting for transfers between devices  317 us (69%)
  local copies, waits for them, and re-layouts  46 us (10%)
  starting transfers between devices  41.3 us (9%)
  Pallas kernels  27.5 us (6%)
  between operations  14.3 us (3%)
  other arithmetic  9.45 us (2%)
    all_to_all x4, waiting for transfers between devices, exchange(): lax.all_to_all(part, 'expert', split_axis=0, concat_axis=0, tiled=True)  112 us
    all_gather x1, waiting for transfers between devices, local(): every = lax.all_gather(arrived, 'dp', axis=0)  110 us
    reduce_scatter x1, waiting for transfers between devices, local(): total = lax.psum_scatter(output, 'dp', scatter_dimension=0)  95.6 us
    all_to_all x4, starting transfers between devices, exchange(): lax.all_to_all(part, 'expert', split_axis=0, concat_axis=0, tiled=True)  38.1 us
    unnamed x28, local copies, waits for them, and re-layouts  30.5 us
    pallas_call x2, Pallas kernels, pick(): pl.pallas_call(lambda *refs: pick_kernel(count, *refs), out_shape=jax.Sha...  15.6 us
    pallas_call x1, Pallas kernels, ffn(): pl.pallas_call(ffn_kernel, out_shape=jax.ShapeDtypeStruct(rows.shape, jnp...  11.9 us
    slice x2, local copies, waits for them, and re-layouts, local(): moved = (back_a[:, :piece], back_a[:, piece:], back_b[:, :piece])  10.8 us
  transfers between devices with their start and end apart: 9, of which 4 were waited for; matrix products, arithmetic and copies ran while one was open for 8% of the time, Pallas kernels for 6%

profile of v2, /device:TPU:1, one launch (start us, length us, event | category | flops | bytes accessed | tf_op | source)
XLA Modules:
  0.0 457.1 jit_solution(10559477801067673558)
XLA Ops:
  7.2 0.7 reduce_sum.18
  7.9 0.7 broadcast_divide_fusion
  8.6 0.7 convert_element_type.18
  9.3 1.4 collective-permute-start
  10.7 0.9 broadcast_select_fusion.3
  11.6 0.1 collective-permute-start.1
  11.7 4.1 constant_dynamic-update-slice_fusion
  15.8 0.1 eq.46
  15.9 0.1 maximum_select_fusion.3
  15.9 0.1 copy.16
  16.0 0.1 fusion.24
  16.1 0.2 fusion.38
  16.3 0.1 copy.17
  16.5 0.5 convolution_convert_fusion
  16.9 0.7 fusion.18
  17.7 0.7 fusion.17
  18.4 0.7 fusion.16
  19.1 0.7 fusion.15
  19.8 0.7 fusion.14
  20.6 0.7 fusion.1
  21.3 11.0 %all-to-all-start = ((bf16[32,176,384]{2,1,0:T(8,128)(2,1)}), bf16[32,176,384]{2,1,0:T(8,128)(2,1)}, u32[]{:S(2)}, u32[]{:S(2)}) async-start(bf16[32,176,384]{2,1,0:T(8,128)(2,1)} %fusion.1), calls=%async_computation | async-start | bytes 8650752 | tf_op jit(solution)/shard_map/all_to_all | solution.py:18
  32.3 0.0 all-gather.3.cloned.1.call-start
  32.4 5.4 %pad_maximum_fusion = bf16[32,256,384]{2,1,0:T(8,128)(2,1)} fusion(bf16[32,128,384]{2,1,0:T(8,128)(2,1)S(1)} %bitcast.122, bf16[32,128,384]{2,1,0:T(8,128)(2,1)} %bitcast.123), kind=kLoop, calls=%fused_computation | loop fusion | flops 12582912 | bytes 12582912 | tf_op jit(solution)/shard_map/concatenate | solution.py:160
  37.8 53.3 %all-to-all-done.refs_1_.refs_3_.refs_5_.refs_7_ = bf16[32,176,384]{2,1,0:T(8,128)(2,1)} async-done(((bf16[32,176,384]{2,1,0:T(8,128)(2,1)}), bf16[32,176,384]{2,1,0:T(8,128)(2,1)}, u32[]{:S(2)}, u32[]{:S(2)}) %all-to-all-start) | async-done | bytes 4325408 | tf_op jit(solution)/shard_map/all_to_all | solution.py:18
  91.0 0.9 slice_bitcast_fusion.16
  92.0 1.0 bitcast_dynamic-update-slice_fusion.4
  93.0 1.0 bitcast_dynamic-update-slice_fusion.3
  93.9 1.0 bitcast_dynamic-update-slice_fusion.2
  94.9 1.0 bitcast_dynamic-update-slice_fusion.1
  95.9 1.0 bitcast_dynamic-update-slice_fusion
  96.9 1.0 copy-done.2
  97.8 0.0 all-gather.3.cloned.1.call-update
  97.9 7.4 %all-to-all-start.1 = ((bf16[32,256,384]{2,1,0:T(8,128)(2,1)}), bf16[32,256,384]{2,1,0:T(8,128)(2,1)}, u32[]{:S(2)}, u32[]{:S(2)}) async-start(bf16[32,256,384]{2,1,0:T(8,128)(2,1)} %pad_maximum_fusion), calls=%async_computation.1 | async-start | bytes 12582912 | tf_op jit(solution)/shard_map/all_to_all | solution.py:18
  105.2 0.0 reduce-scatter.2.cloned.1.call-start
  105.3 109.7 %all-gather.3.cloned.1.call-done = bf16[1024,2048]{1,0:T(8,128)(2,1)} async-done(((bf16[256,2048]{1,0:T(8,128)(2,1)}), bf16[1024,2048]{1,0:T(8,128)(2,1)}) %all-gather.3.cloned.1.call-update) | async-done | bytes 4194320 | tf_op jit(solution)/shard_map/all_gather | solution.py:165
  215.0 11.9 %ffn.1 = bf16[4,256,2048]{2,1,0:T(8,128)(2,1)} custom-call(bf16[4,256,2048]{2,1,0:T(8,128)(2,1)} %bitcast.127, bf16[4096,384]{1,0:T(8,128)(2,1)S(1)} %bitcast.113, bf16[4096,384]{1,0:T(8,128)(2,1)} %bitcast.124, bf16[4096,384]{1,0:T(8,128)(2,1)} %bitcast.121), custom_call_target="tpu_custom_call" | custom-call | flops 4831838208 | bytes 17825792 | tf_op jit(solution)/shard_map/ffn/pallas_call | solution.py:108
  226.9 0.0 reduce-scatter.2.cloned.1.call-update
  226.9 8.6 %pick.2 = bf16[32,256,384]{2,1,0:T(8,128)(2,1)} custom-call(s32[32]{0:T(128)} %refs_0_.3, bf16[32,176,384]{2,1,0:T(8,128)(2,1)} %all-to-all-done.refs_1_.refs_3_.refs_5_.refs_7_, bf16[32,256,384]{2,1,0:T(8,128)(2,1)} %all-to-all-done.1.refs_2_.refs_4_.refs_6_.refs_8_.refs_1_.refs_3_, bf16[32,176,384]{2,1,0:T(8,128)(2,1)} %all-to-all-done.refs_1_.refs_3_.refs_5_.refs_7_, ...), custom_call_target="tpu_custom_call" | custom-call | bytes 12582912 | tf_op jit(solution)/shard_map/pick/pallas_call | solution.py:67
  235.6 10.8 %all-to-all-start.2 = ((bf16[32,256,384]{2,1,0:T(8,128)(2,1)}), bf16[32,256,384]{2,1,0:T(8,128)(2,1)}, u32[]{:S(2)}, u32[]{:S(2)}) async-start(bf16[32,256,384]{2,1,0:T(8,128)(2,1)} %pick.2), calls=%async_computation.2 | async-start | bytes 12582912 | tf_op jit(solution)/shard_map/all_to_all | solution.py:18
  246.4 7.0 %pick.3 = bf16[32,128,384]{2,1,0:T(8,128)(2,1)} custom-call(s32[32]{0:T(128)} %refs_0_.3, bf16[32,256,384]{2,1,0:T(8,128)(2,1)} %all-to-all-done.1.refs_2_.refs_4_.refs_6_.refs_8_.refs_1_.refs_3_, bf16[32,256,384]{2,1,0:T(8,128)(2,1)} %all-to-all-done.1.refs_2_.refs_4_.refs_6_.refs_8_.refs_1_.refs_3_, ...), custom_call_target="tpu_custom_call" | custom-call | bytes 6291456 | tf_op jit(solution)/shard_map/pick/pallas_call | solution.py:67
  253.4 4.0 constant_dynamic-update-slice_fusion.1
  257.4 95.6 %reduce-scatter.2.cloned.1.call-done = bf16[1,256,2048]{2,1,0:T(8,128)(2,1)} async-done(((bf16[4,256,2048]{2,1,0:T(8,128)(2,1)}), bf16[1,256,2048]{2,1,0:T(8,128)(2,1)}) %reduce-scatter.2.cloned.1.call-update) | async-done | bytes 1048592 | tf_op jit(solution)/shard_map/reduce_scatter | solution.py:167
  353.1 1.7 fusion.13
  354.8 1.6 fusion.12
  356.4 1.6 fusion.11
  358.0 1.6 fusion.10
  359.7 1.6 fusion.9
  361.3 1.6 fusion.3
  362.9 8.9 %all-to-all-start.3 = ((bf16[32,176,384]{2,1,0:T(8,128)(2,1)}), bf16[32,176,384]{2,1,0:T(8,128)(2,1)}, u32[]{:S(2)}, u32[]{:S(2)}) async-start(bf16[32,176,384]{2,1,0:T(8,128)(2,1)} %fusion.3), calls=%async_computation.4 | async-start | bytes 8650752 | tf_op jit(solution)/shard_map/all_to_all | solution.py:18
  371.8 0.1 copy.19
  371.9 0.1 select_reduce_fusion
  372.0 0.1 copy.20
  372.1 58.4 %all-to-all-done.3 = bf16[32,176,384]{2,1,0:T(8,128)(2,1)} async-done(((bf16[32,176,384]{2,1,0:T(8,128)(2,1)}), bf16[32,176,384]{2,1,0:T(8,128)(2,1)}, u32[]{:S(2)}, u32[]{:S(2)}) %all-to-all-start.3) | async-done | bytes 4325408 | tf_op jit(solution)/shard_map/all_to_all | solution.py:18
  430.6 0.9 slice_bitcast_fusion
  431.5 1.0 fusion.8
  432.5 1.0 fusion.7
  433.4 1.0 fusion.6
  434.4 1.0 fusion.5
  435.4 1.0 fusion.4
  436.4 0.8 convolution_convert_fusion.1
  437.2 1.6 collective-permute-start.2
  438.8 6.7 %fusion.47 = (bf16[32,128,384]{2,1,0:T(8,128)(2,1)}, bf16[32,128,384]{2,1,0:T(8,128)(2,1)}) fusion(bf16[32,256,384]{2,1,0:T(8,128)(2,1)} %all-to-all-done.2), kind=kLoop, calls=%fused_computation.91 | loop fusion | bytes 12582912 | tf_op jit(solution)/shard_map/slice | solution.py:189
  445.5 4.1 slice.188
  449.6 0.7 maximum_select_fusion.2
  (17 shorter events, 0.1 us)
Async XLA Ops:
  9.3 6.6 %collective-permute-start = (f32[16,16]{0,1:T(8,128)S(1)}, f32[16,16]{0,1:T(8,128)S(1)}, u32[]{:S(2)}, u32[]{:S(2)}) collective-permute-start(f32[16,16]{0,1:T(8,128)S(1)} %pad_maximum_fusion.1), channel_id=1, source_target_pairs={{0,32},{32,0},{64,96},{96,64},{1,33},{33,1},{65,97},{97,65},{2,34}... | collective-permute-start | bytes 3080 | tf_op jit(solution)/shard_map/ppermute | solution.py:14
  11.6 4.9 %collective-permute-start.1 = (bf16[16,2048]{1,0:T(8,128)(2,1)S(1)}, bf16[16,2048]{1,0:T(8,128)(2,1)S(1)}, u32[]{:S(2)}, u32[]{:S(2)}) collective-permute-start(bf16[16,2048]{1,0:T(8,128)(2,1)S(1)} %get-tuple-element.17), channel_id=1, source_target_pairs={{0,32},{32,0},{64,96},{96,64},{1,33},{33,1},{65,97},{97,65},{2,34}... | collective-permute-start | bytes 196616 | tf_op jit(solution)/shard_map/ppermute | solution.py:14
  21.3 11.0 %copy-start.1 = (bf16[1,4096,384]{2,1,0:T(8,128)(2,1)S(1)}, bf16[1,4096,384]{2,1,0:T(8,128)(2,1)}, u32[]{:S(2)}) copy-start(bf16[1,4096,384]{2,1,0:T(8,128)(2,1)} %param.13) | copy-start | bytes 9437188
  21.3 69.7 %all-to-all-start = ((bf16[32,176,384]{2,1,0:T(8,128)(2,1)}), bf16[32,176,384]{2,1,0:T(8,128)(2,1)}, u32[]{:S(2)}, u32[]{:S(2)}) async-start(bf16[32,176,384]{2,1,0:T(8,128)(2,1)} %fusion.1), calls=%async_computation | async-start | bytes 8650752 | tf_op jit(solution)/shard_map/all_to_all | solution.py:18
  32.3 182.7 %all-gather.3.cloned.1.call-start = ((), (), s32[]{:S(2)}) async-start(), calls=%async_computation.6 | async-start | bytes 5242880 | tf_op jit(solution)/shard_map/all_gather | solution.py:165
  96.9 1.0 copy-start.2
  97.9 117.1 %copy-start = (bf16[1,4096,384]{2,1,0:T(8,128)(2,1)S(1)}, bf16[1,4096,384]{2,1,0:T(8,128)(2,1)}, u32[]{:S(2)}) copy-start(bf16[1,4096,384]{2,1,0:T(8,128)(2,1)} %param.11) | copy-start | bytes 9437188
  97.9 129.1 %all-to-all-start.1 = ((bf16[32,256,384]{2,1,0:T(8,128)(2,1)}), bf16[32,256,384]{2,1,0:T(8,128)(2,1)}, u32[]{:S(2)}, u32[]{:S(2)}) async-start(bf16[32,256,384]{2,1,0:T(8,128)(2,1)} %pad_maximum_fusion), calls=%async_computation.1 | async-start | bytes 12582912 | tf_op jit(solution)/shard_map/all_to_all | solution.py:18
  105.2 247.8 %reduce-scatter.2.cloned.1.call-start = ((), (), s32[]{:S(2)}) async-start(), calls=%async_computation.5 | async-start | bytes 5242880 | tf_op jit(solution)/shard_map/reduce_scatter | solution.py:167
  235.6 127.3 %all-to-all-start.2 = ((bf16[32,256,384]{2,1,0:T(8,128)(2,1)}), bf16[32,256,384]{2,1,0:T(8,128)(2,1)}, u32[]{:S(2)}, u32[]{:S(2)}) async-start(bf16[32,256,384]{2,1,0:T(8,128)(2,1)} %pick.2), calls=%async_computation.2 | async-start | bytes 12582912 | tf_op jit(solution)/shard_map/all_to_all | solution.py:18
  362.9 67.7 %all-to-all-start.3 = ((bf16[32,176,384]{2,1,0:T(8,128)(2,1)}), bf16[32,176,384]{2,1,0:T(8,128)(2,1)}, u32[]{:S(2)}, u32[]{:S(2)}) async-start(bf16[32,176,384]{2,1,0:T(8,128)(2,1)} %fusion.3), calls=%async_computation.4 | async-start | bytes 8650752 | tf_op jit(solution)/shard_map/all_to_all | solution.py:18
  437.2 12.4 %collective-permute-start.2 = (bf16[16,2048]{1,0:T(8,128)(2,1)S(1)}, bf16[16,2048]{1,0:T(8,128)(2,1)S(1)}, u32[]{:S(2)}, u32[]{:S(2)}) collective-permute-start(bf16[16,2048]{1,0:T(8,128)(2,1)S(1)} %get-tuple-element.15), channel_id=1, source_target_pairs={{0,32},{32,0},{64,96},{96,64},{1,33},{33,1},{65,97},{97,65},{2,34}... | collective-permute-start | bytes 196616 | tf_op jit(solution)/shard_map/ppermute | solution.py:14
Sparse Core Ops, SparseCore 0:
  98.0 116.9 all-gather.2
  227.1 125.9 reduce-scatter.1
